TPU v7x, 256 devices: a whole 4x4x8 slice. The times are simulated.
256 devices in a mesh: section: 2 (over z_hi), gy: 32 (over z_lo, x, core), gz: 4 (over y).
Axes of the slice: x: 4, y: 4, z: 8 (z_hi: 2, z_lo: 4; z = z_hi * 4 + z_lo), core: 2. Of those that a mesh axis runs over, the one named last changes fastest.
Arguments:
- inflow: float32 [2, 64, 2, 64, 512], P(None, None, None, 'gy', 'gz'), may hold values from -6 to 6
- weights: float32 [4, 27, 64, 64], P('section'), may hold values from -0.15625 to 0.15625
- biases: float32 [4, 64], P('section'), may hold values from -3 to 3
- cotangent: float32 [2, 64, 2, 64, 512], P(None, None, None, 'gy', 'gz'), may hold values from -6 to 6
Outputs:
- section_out: float32 [2, 2, 64, 2, 64, 512], P('section', None, None, None, 'gy', 'gz')
- section_grad: float32 [2, 2, 64, 2, 64, 512], P('section', None, None, None, 'gy', 'gz')
- weight_grad: float32 [4, 27, 64, 64], P('section')
- bias_grad: float32 [4, 64], P('section')
All inputs are finite; a program needn't handle non-finite values.
Results may differ from a plain program's by a relative error of at most 0.0001.
Values sent between devices are 32-bit elements; how exact they have to be, the bound alone decides.
A program may use at most 128 MiB of HBM per device.

v0:
```python
import math
import jax
import jax.numpy as jnp
from jax import lax
from jax.sharding import PartitionSpec as P


def extended(block, sides, width):
    for axis, dim in sides:
        count = lax.axis_size(axis)
        forward = [(i, i + 1) for i in range(count - 1)]
        backward = [(target, source) for source, target in forward]
        low = lax.ppermute(
            lax.slice_in_dim(block, block.shape[dim] - width, None, axis=dim), axis, forward
        )
        high = lax.ppermute(lax.slice_in_dim(block, 0, width, axis=dim), axis, backward)
        block = jnp.concatenate([low, block, high], axis=dim)
    return block


def passed_along(block, axis, distance):
    devices = range(lax.axis_size(axis))
    route = [(i - distance, i) for i in devices if i - distance in devices]
    return lax.ppermute(block, axis, route)


def stacked_taps(padded, out_sizes, flipped):
    size_x, size_y, size_z = out_sizes
    pieces = []
    for offset in range(27):
        start_x, start_y, start_z = (offset // 9, offset // 3 % 3, offset % 3)
        if flipped:
            start_x, start_y, start_z = (2 - start_x, 2 - start_y, 2 - start_z)
        pieces.append(
            padded[
                :,
                start_x : start_x + size_x,
                start_y : start_y + size_y,
                start_z : start_z + size_z,
            ]
        )
    return jnp.stack(pieces)


def convolve(weight, padded, out_sizes):
    return jnp.einsum(
        "toc,tcxyz->oxyz",
        weight,
        stacked_taps(padded, out_sizes, False),
        precision=lax.Precision.HIGHEST,
    )


def face_rim(values):
    rimmed = extended(values, (("gy", 2), ("gz", 3)), 1)
    return jnp.pad(rimmed, ((0, 0), (1, 1), (0, 0), (0, 0)))


def slope_rim(values):
    rimmed = extended(values, (("gy", 2), ("gz", 3)), 1)
    return jnp.pad(rimmed, ((0, 0), (1, 1), (0, 0), (0, 0)))


def section_forward(weights, biases, current, extents):
    stored = []
    for layer_index in range(weights.shape[0]):
        padded = face_rim(current)
        pre_act = (
            convolve(weights[layer_index], padded, extents)
            + biases[layer_index][:, None, None, None]
        )
        stored.append((padded, pre_act))
        current = jax.nn.silu(pre_act)
    return (stored, current)


def per_device(inflow, weights, biases, cotangent):
    highest = lax.Precision.HIGHEST
    first_section = lax.axis_index("section") == 0
    micro_count = inflow.shape[0]
    layer_count = weights.shape[0]
    extents = inflow.shape[2:]
    blank = jnp.zeros(inflow.shape[1:], jnp.float32)
    received = blank
    stored_all = []
    produced = []
    for step_index in range(micro_count + 1):
        own_input = inflow[step_index] if step_index < micro_count else blank
        current = jnp.where(first_section, own_input, received)
        stored, current = section_forward(weights, biases, current, extents)
        stored_all.append(stored)
        produced.append(current)
        if step_index < micro_count:
            received = passed_along(current, "section", 1)
    section_out = jnp.stack(
        [
            jnp.where(first_section, produced[micro], produced[micro + 1])
            for micro in range(micro_count)
        ]
    )
    cell_count = (
        micro_count
        * extents[0]
        * extents[1]
        * lax.axis_size("gy")
        * extents[2]
        * lax.axis_size("gz")
    )
    grad_scale = 1.0 / math.sqrt(cell_count)
    weight_grads = [jnp.zeros(weights.shape[1:], jnp.float32) for layer_index in range(layer_count)]
    bias_grads = [jnp.zeros(biases.shape[1:], jnp.float32) for layer_index in range(layer_count)]
    returned = blank
    collected = []
    for step_index in range(micro_count + 1):
        later = micro_count - 1 - step_index
        own_grad = cotangent[later] if later >= 0 else blank
        gradient = jnp.where(first_section, returned, own_grad)
        stored = stored_all[micro_count - step_index]
        for layer_index in reversed(range(layer_count)):
            padded, pre_act = stored[layer_index]
            sigmoid_value = jax.nn.sigmoid(pre_act)
            slope_grad = gradient * sigmoid_value * (1.0 + pre_act * (1.0 - sigmoid_value))
            weight_grads[layer_index] = weight_grads[layer_index] + jnp.einsum(
                "oxyz,tcxyz->toc",
                slope_grad,
                stacked_taps(padded, extents, False),
                precision=highest,
            )
            bias_grads[layer_index] = bias_grads[layer_index] + jnp.sum(slope_grad, axis=(1, 2, 3))
            gradient = jnp.einsum(
                "toc,toxyz->cxyz",
                weights[layer_index],
                stacked_taps(slope_rim(slope_grad), extents, True),
                precision=highest,
            )
        collected.append(gradient)
        if step_index < micro_count:
            returned = passed_along(gradient, "section", -1)
    section_grad = jnp.stack(
        [
            jnp.where(
                first_section, collected[micro_count - micro], collected[micro_count - 1 - micro]
            )
            for micro in range(micro_count)
        ]
    )
    weight_total, bias_total = lax.psum(
        (jnp.stack(weight_grads) * grad_scale, jnp.stack(bias_grads) * grad_scale), ("gy", "gz")
    )
    return (section_out[None], section_grad[None], weight_total, bias_total)


def solution(mesh):
    return jax.shard_map(
        per_device,
        mesh=mesh,
        in_specs=(
            P(None, None, None, "gy", "gz"),
            P("section", None, None, None),
            P("section", None),
            P(None, None, None, "gy", "gz"),
        ),
        out_specs=(
            P("section", None, None, None, "gy", "gz"),
            P("section", None, None, None, "gy", "gz"),
            P("section", None, None, None),
            P("section", None),
        ),
        check_vma=False,
    )
```

profile of v0, /device:TPU:8, one launch (start us, length us, event | category | flops | bytes accessed | tf_op | source)
XLA Modules:
  0.0 1630.1 jit_solution(7726312461387545481)
XLA Ops:
  11.3 3.1 collective-permute-done.1
  14.6 3.5 collective-permute-start.2
  23.6 3.8 collective-permute-done.3
  32.4 3.5 collective-permute-start.4
  37.2 4.1 collective-permute-done.5
  41.4 3.2 collective-permute-start.6
  47.3 3.2 collective-permute-done.6
  50.5 3.5 collective-permute-done.7
  59.0 9.1 collective-permute-start.8
  68.1 3.3 collective-permute-done.8
  75.4 4.7 collective-permute-done.10
  82.2 4.2 collective-permute-start.12
  96.2 3.8 collective-permute-start.13
  101.3 4.0 collective-permute-done.14
  107.7 3.7 collective-permute-start.16
  111.3 3.2 collective-permute-done.15
  122.1 8.2 collective-permute-start.17
  130.3 3.2 collective-permute-done.17
  137.6 3.2 collective-permute-done.19
  143.2 3.7 collective-permute-start.21
  146.8 3.2 collective-permute-done.20
  157.5 3.5 collective-permute-start.22
  162.3 4.1 collective-permute-done.23
  168.5 4.4 collective-permute-start.25
  182.8 3.8 collective-permute-start.26
  187.9 3.3 collective-permute-done.27
  193.3 3.9 collective-permute-start.29
  197.2 3.2 collective-permute-done.28
  207.2 3.8 collective-permute-start.30
  212.2 3.8 collective-permute-done.31
  218.2 3.9 collective-permute-start.33
  222.1 3.2 collective-permute-done.32
  233.2 10.2 collective-permute-done.34
  247.7 4.6 collective-permute-done.36
  254.8 3.6 collective-permute-start.38
  269.0 3.5 collective-permute-start.39
  278.4 3.7 collective-permute-start.42
  293.9 3.0 fusion.24
  296.9 7.1 collective-permute-done.43
  304.2 3.0 convolution_bitcast_fusion
  310.8 3.0 fusion.27
  316.8 4.2 collective-permute-start.47
  330.6 3.0 fusion.23
  335.1 3.8 collective-permute-start.48
  340.2 3.6 collective-permute-done.49
  345.9 3.9 collective-permute-start.51
  349.8 333.4 %psum.15 = f32[2,64]{1,0:T(2,128)} all-reduce(f32[2,64]{1,0:T(2,128)S(1)} %maximum_multiply_fusion.1), channel_id=1, replica_groups=mesh['section'=2,'gy'=32,'gz'=4] {'gy','gz'}, use_global_device_ids=true, to_apply=%region_7.8 | all-reduce | flops 128 | bytes 1024 | tf_op jit(solution)/shard_map/psum | solution.py:147
  688.9 931.3 %all-reduce.14.cloned.1.call-done = f32[2,27,64,64]{2,3,1,0:T(8,128)} async-done(((f32[2,27,64,64]{2,3,1,0:T(8,128)}), f32[2,27,64,64]{2,3,1,0:T(8,128)}) %all-reduce.14.cloned.1.call-update) | async-done | bytes 884752 | tf_op jit(solution)/shard_map/psum | solution.py:147
  (482 shorter events, 161.3 us)
Async XLA Ops:
  7.2 1613.0 %all-reduce.14.cloned.1.call-start = ((), (), s32[]{:S(2)}) async-start(), calls=%async_computation | async-start | bytes 3538944 | tf_op jit(solution)/shard_map/psum | solution.py:147
  10.0 4.4 collective-permute-start.1
  14.6 9.0 collective-permute-start.2
  18.1 9.3 collective-permute-start.3
  32.4 4.8 collective-permute-start.4
  35.9 5.4 collective-permute-start.5
  41.4 9.0 collective-permute-start.6
  44.6 9.3 collective-permute-start.7
  59.0 12.4 collective-permute-start.8
  74.0 6.0 collective-permute-start.10
  80.2 9.0 collective-permute-start.11
  82.2 9.0 collective-permute-start.12
  96.2 5.1 collective-permute-start.13
  100.0 5.3 collective-permute-start.14
  105.5 9.0 collective-permute-start.15
  107.7 9.3 collective-permute-start.16
  122.1 11.4 collective-permute-start.17
  136.3 4.5 collective-permute-start.19
  141.0 9.0 collective-permute-start.20
  143.2 9.3 collective-permute-start.21
  157.5 4.8 collective-permute-start.22
  161.0 5.4 collective-permute-start.23
  166.6 9.0 collective-permute-start.24
  168.5 9.0 collective-permute-start.25
  182.8 5.1 collective-permute-start.26
  186.6 4.6 collective-permute-start.27
  191.3 9.0 collective-permute-start.28
  193.3 9.0 collective-permute-start.29
  207.2 5.1 collective-permute-start.30
  210.9 5.1 collective-permute-start.31
  216.2 9.0 collective-permute-start.32
  218.2 9.1 collective-permute-start.33
  231.9 11.5 collective-permute-start.34
  246.4 5.9 collective-permute-start.36
  252.4 9.0 collective-permute-start.37
  254.8 9.3 collective-permute-start.38
  269.0 5.7 collective-permute-start.39
  276.3 9.0 collective-permute-start.41
  278.4 9.3 collective-permute-start.42
  292.4 11.6 collective-permute-start.43
  307.2 6.6 collective-permute-start.44
  309.5 5.1 collective-permute-start.45
  314.8 9.0 collective-permute-start.46
  316.8 9.0 collective-permute-start.47
  335.1 5.1 collective-permute-start.48
  338.9 4.9 collective-permute-start.49
  344.0 339.3 %collective-permute-start.50 = (f32[64,2,4,1]{3,0,2,1:T(8,128)S(1)}, f32[64,2,4,1]{3,0,2,1:T(8,128)S(1)}, u32[]{:S(2)}, u32[]{:S(2)}) collective-permute-start(f32[64,2,4,1]{3,0,2,1:T(8,128)S(1)} %get-tuple-element.22), channel_id=1, source_target_pairs={{0,1},{1,2},{2,3},{4,5},{5,6},{6,7},{8,9},{9,10},{10,11},{12,13},{... | collective-permute-start | bytes 6152 | tf_op jit(solution)/shard_map/ppermute | solution.py:13
  345.9 337.4 %collective-permute-start.51 = (f32[64,2,4,1]{3,0,2,1:T(8,128)S(1)}, f32[64,2,4,1]{3,0,2,1:T(8,128)S(1)}, u32[]{:S(2)}, u32[]{:S(2)}) collective-permute-start(f32[64,2,4,1]{3,0,2,1:T(8,128)S(1)} %get-tuple-element.23), channel_id=1, source_target_pairs={{1,0},{2,1},{3,2},{5,4},{6,5},{7,6},{9,8},{10,9},{11,10},{13,12},{... | collective-permute-start | bytes 6152 | tf_op jit(solution)/shard_map/ppermute | solution.py:16
  (7 other events, 38.3 us)
Sparse Core Ops, SparseCore 0:
  335.3 1284.8 all-reduce.13
where the time goes:
time: 1640 us; the launch traced here: 1630 us
  waiting for transfers between devices  1050 us (64%)
  blocking collectives  333 us (20%)
  starting transfers between devices  144 us (9%)
  matrix products  46.1 us (3%)
  local copies, waits for them, and re-layouts  22.3 us (1%)
  between operations  18 us (1%)
    psum x1, waiting for transfers between devices, per_device(): lax.psum((jnp.stack(weight_grads) * grad_scale, jnp.stack(bias_grads) * g...  931 us
    psum x1, blocking collectives, per_device(): lax.psum((jnp.stack(weight_grads) * grad_scale, jnp.stack(bias_grads) * g...  333 us
    ppermute x24, waiting for transfers between devices, extended(): lax.ppermute(lax.slice_in_dim(block, 0, width, axis=dim), axis, backward)  67.7 us
    ppermute x24, starting transfers between devices, extended(): lax.ppermute(lax.slice_in_dim(block, block.shape[dim] - width, None, axis...  64.7 us
    ppermute x24, starting transfers between devices, extended(): lax.ppermute(lax.slice_in_dim(block, 0, width, axis=dim), axis, backward)  59.7 us
  transfers between devices with their start and end apart: 53, of which 38 were waited for; matrix products, arithmetic and copies ran while one was open for 1% of the time, Pallas kernels for 0%

commit v1 on v0

--- a/solution.py
+++ b/solution.py
@@ -145,7 +145,8 @@
         ]
     )
     weight_total, bias_total = lax.psum(
-        (jnp.stack(weight_grads) * grad_scale, jnp.stack(bias_grads) * grad_scale), ("gy", "gz")
+        lax.psum((jnp.stack(weight_grads) * grad_scale, jnp.stack(bias_grads) * grad_scale), "gy"),
+        "gz",
     )
     return (section_out[None], section_grad[None], weight_total, bias_total)
 

time: 1640 us -> 698 us (0.43)
  waiting for transfers between devices: 1050 us -> 340 us
  blocking collectives: 333 us -> 77.7 us
    psum x1, waiting for transfers between devices: 931 us -> 169 us  [per_device(): lax.psum((jnp.stack(weight_grads) * grad_scale, jnp.stack(bias_grads) * g...]
    psum x1, blocking collectives: 333 us -> 69.7 us  [per_device(): lax.psum((jnp.stack(weight_grads) * grad_scale, jnp.stack(bias_grads) * g...]
    psum x0 -> x1, waiting for transfers between devices: none -> 52.7 us  [per_device(): lax.psum(lax.psum((jnp.stack(weight_grads) * grad_scale, jnp.stack(bias_g...]
  transfers between devices with their start and end apart: 53 -> 54, of which waited for: 38 -> 39; matrix products, arithmetic and copies ran while one was open for 1% -> 6% of each run, Pallas kernels for 0% -> 0%
where the time goes in v1:
time: 698 us; the launch traced here: 688 us
  waiting for transfers between devices  340 us (49%)
  starting transfers between devices  145 us (21%)
  blocking collectives  77.7 us (11%)
  matrix products  48.1 us (7%)
  local copies, waits for them, and re-layouts  34.8 us (5%)
  other arithmetic  24.8 us (4%)
  between operations  17.8 us (3%)
    psum x1, waiting for transfers between devices, per_device(): lax.psum((jnp.stack(weight_grads) * grad_scale, jnp.stack(bias_grads) * g...  169 us
    psum x1, blocking collectives, per_device(): lax.psum((jnp.stack(weight_grads) * grad_scale, jnp.stack(bias_grads) * g...  69.7 us
    ppermute x24, waiting for transfers between devices, extended(): lax.ppermute(lax.slice_in_dim(block, 0, width, axis=dim), axis, backward)  67.8 us
    ppermute x24, starting transfers between devices, extended(): lax.ppermute(lax.slice_in_dim(block, block.shape[dim] - width, None, axis...  64.7 us
    ppermute x24, starting transfers between devices, extended(): lax.ppermute(lax.slice_in_dim(block, 0, width, axis=dim), axis, backward)  59.7 us
    psum x1, waiting for transfers between devices, per_device(): lax.psum(lax.psum((jnp.stack(weight_grads) * grad_scale, jnp.stack(bias_g...  52.7 us
    unnamed x222, local copies, waits for them, and re-layouts  30 us
    ppermute x24, waiting for transfers between devices, extended(): lax.ppermute(lax.slice_in_dim(block, block.shape[dim] - width, None, axis...  27 us
  transfers between devices with their start and end apart: 54, of which 39 were waited for; matrix products, arithmetic and copies ran while one was open for 6% of the time, Pallas kernels for 0%

profile of v1, /device:TPU:8, one launch (start us, length us, event | category | flops | bytes accessed | tf_op | source)
XLA Modules:
  0.0 687.9 jit_solution(15714478837259856900)
XLA Ops:
  11.3 3.1 collective-permute-done.1
  14.6 3.5 collective-permute-start.2
  23.6 3.8 collective-permute-done.3
  32.4 3.5 collective-permute-start.4
  37.2 4.1 collective-permute-done.5
  41.4 3.2 collective-permute-start.6
  47.3 3.2 collective-permute-done.6
  50.5 3.5 collective-permute-done.7
  59.0 9.1 %collective-permute-start.8 = (f32[64,2,2,128]{3,0,2,1:T(8,128)S(1)}, f32[64,2,2,128]{3,0,2,1:T(8,128)S(1)}, u32[]{:S(2)}, u32[]{:S(2)}) collective-permute-start(f32[64,2,2,128]{3,0,2,1:T(8,128)S(1)} %bitcast_multiply_fusion.12), channel_id=1, source_target_pairs={{0,128},{1,129},{2,130},{3,131},{4,132},{5,133},{6,134},{7,135},{8... | collective-permute-start | bytes 393224 | tf_op jit(solution)/shard_map/ppermute | solution.py:24
  68.1 3.3 collective-permute-done.8
  75.4 4.7 collective-permute-done.10
  82.2 4.2 collective-permute-start.12
  96.2 3.8 collective-permute-start.13
  101.3 4.0 collective-permute-done.14
  107.7 3.7 collective-permute-start.16
  111.3 3.2 collective-permute-done.15
  122.2 8.2 %collective-permute-start.17 = (f32[64,2,2,128]{3,0,2,1:T(8,128)S(1)}, f32[64,2,2,128]{3,0,2,1:T(8,128)S(1)}, u32[]{:S(2)}, u32[]{:S(2)}) collective-permute-start(f32[64,2,2,128]{3,0,2,1:T(8,128)S(1)} %get-tuple-element.21), channel_id=1, source_target_pairs={{0,128},{1,129},{2,130},{3,131},{4,132},{5,133},{6,134},{7,135},{8... | collective-permute-start | bytes 393224 | tf_op jit(solution)/shard_map/ppermute | solution.py:24
  130.3 3.2 collective-permute-done.17
  137.6 3.2 collective-permute-done.19
  143.2 3.7 collective-permute-start.21
  146.8 3.2 collective-permute-done.20
  157.6 3.5 collective-permute-start.22
  162.4 4.1 collective-permute-done.23
  168.5 4.4 collective-permute-start.25
  182.8 3.8 collective-permute-start.26
  187.9 3.3 collective-permute-done.27
  193.3 3.9 collective-permute-start.29
  197.2 3.2 collective-permute-done.28
  207.2 3.8 collective-permute-start.30
  212.3 3.8 collective-permute-done.31
  218.2 3.9 collective-permute-start.33
  222.1 3.2 collective-permute-done.32
  233.2 10.2 %collective-permute-done.34 = f32[64,2,2,128]{3,0,2,1:T(8,128)S(1)} collective-permute-done((f32[64,2,2,128]{3,0,2,1:T(8,128)S(1)}, f32[64,2,2,128]{3,0,2,1:T(8,128)S(1)}, u32[]{:S(2)}, u32[]{:S(2)}) %collective-permute-start.34) | collective-permute-done | bytes 131104 | tf_op jit(solution)/shard_map/ppermute | solution.py:24
  247.7 4.6 collective-permute-done.36
  254.8 3.6 collective-permute-start.38
  269.0 3.5 collective-permute-start.39
  278.4 3.7 collective-permute-start.42
  296.9 7.0 %collective-permute-done.43 = f32[64,2,2,128]{3,0,2,1:T(8,128)S(1)} collective-permute-done((f32[64,2,2,128]{3,0,2,1:T(8,128)S(1)}, f32[64,2,2,128]{3,0,2,1:T(8,128)S(1)}, u32[]{:S(2)}, u32[]{:S(2)}) %collective-permute-start.43) | collective-permute-done | bytes 131104 | tf_op jit(solution)/shard_map/ppermute | solution.py:24
  316.8 4.2 collective-permute-start.47
  330.6 3.0 fusion.23
  335.2 3.8 collective-permute-start.48
  340.3 3.6 collective-permute-done.49
  345.9 3.9 collective-permute-start.51
  349.9 69.7 %psum.30 = f32[2,64]{1,0:T(2,128)S(1)} all-reduce(f32[2,64]{1,0:T(2,128)S(1)} %maximum_multiply_fusion.1), channel_id=1, replica_groups=mesh['section'=2,'gy'=32,'gz'=4] {'gy'}, use_global_device_ids=true, to_apply=%region_8.9 | all-reduce | flops 128 | bytes 1024 | tf_op jit(solution)/shard_map/psum | solution.py:148
  419.6 7.9 %psum.31 = f32[2,64]{1,0:T(2,128)} all-reduce(f32[2,64]{1,0:T(2,128)S(1)} %psum.30), channel_id=1, replica_groups=mesh['section'=2,'gy'=32,'gz'=4] {'gz'}, use_global_device_ids=true, to_apply=%region_9.10 | all-reduce | flops 128 | bytes 1024 | tf_op jit(solution)/shard_map/psum | solution.py:147
  450.5 168.9 %all-reduce.15.cloned.1.call-done = f32[2,27,64,64]{2,3,1,0:T(8,128)} async-done(((f32[2,27,64,64]{2,3,1,0:T(8,128)}), f32[2,27,64,64]{2,3,1,0:T(8,128)}) %all-reduce.15.cloned.1.call-update) | async-done | bytes 884752 | tf_op jit(solution)/shard_map/psum | solution.py:148
  620.1 4.1 fusion
  625.3 52.7 %all-reduce.17.cloned.1.call-done = f32[2,27,64,64]{2,3,1,0:T(8,128)} async-done(((f32[2,27,64,64]{2,3,1,0:T(8,128)}), f32[2,27,64,64]{2,3,1,0:T(8,128)}) %all-reduce.17.cloned.1.call-update) | async-done | bytes 884752 | tf_op jit(solution)/shard_map/psum | solution.py:147
  (490 shorter events, 189.6 us)
Async XLA Ops:
  7.2 612.3 %all-reduce.15.cloned.1.call-start = ((), (), s32[]{:S(2)}) async-start(), calls=%async_computation | async-start | bytes 3538944 | tf_op jit(solution)/shard_map/psum | solution.py:148
  14.6 9.0 %collective-permute-start.2 = (f32[64,2,4,1]{3,0,2,1:T(8,128)S(1)}, f32[64,2,4,1]{3,0,2,1:T(8,128)S(1)}, u32[]{:S(2)}, u32[]{:S(2)}) collective-permute-start(f32[64,2,4,1]{3,0,2,1:T(8,128)S(1)} %get-tuple-element.48), channel_id=1, source_target_pairs={{0,1},{1,2},{2,3},{4,5},{5,6},{6,7},{8,9},{9,10},{10,11},{12,13},{... | collective-permute-start | bytes 6152 | tf_op jit(solution)/shard_map/ppermute | solution.py:13
  18.1 9.3 %collective-permute-start.3 = (f32[64,2,4,1]{3,0,2,1:T(8,128)S(1)}, f32[64,2,4,1]{3,0,2,1:T(8,128)S(1)}, u32[]{:S(2)}, u32[]{:S(2)}) collective-permute-start(f32[64,2,4,1]{3,0,2,1:T(8,128)S(1)} %get-tuple-element.49), channel_id=1, source_target_pairs={{1,0},{2,1},{3,2},{5,4},{6,5},{7,6},{9,8},{10,9},{11,10},{13,12},{... | collective-permute-start | bytes 6152 | tf_op jit(solution)/shard_map/ppermute | solution.py:16
  32.4 4.8 collective-permute-start.4
  35.9 5.4 collective-permute-start.5
  41.4 9.0 %collective-permute-start.6 = (f32[64,2,4,1]{3,0,2,1:T(8,128)S(1)}, f32[64,2,4,1]{3,0,2,1:T(8,128)S(1)}, u32[]{:S(2)}, u32[]{:S(2)}) collective-permute-start(f32[64,2,4,1]{3,0,2,1:T(8,128)S(1)} %get-tuple-element.46), channel_id=1, source_target_pairs={{0,1},{1,2},{2,3},{4,5},{5,6},{6,7},{8,9},{9,10},{10,11},{12,13},{... | collective-permute-start | bytes 6152 | tf_op jit(solution)/shard_map/ppermute | solution.py:13
  44.6 9.3 %collective-permute-start.7 = (f32[64,2,4,1]{3,0,2,1:T(8,128)S(1)}, f32[64,2,4,1]{3,0,2,1:T(8,128)S(1)}, u32[]{:S(2)}, u32[]{:S(2)}) collective-permute-start(f32[64,2,4,1]{3,0,2,1:T(8,128)S(1)} %get-tuple-element.47), channel_id=1, source_target_pairs={{1,0},{2,1},{3,2},{5,4},{6,5},{7,6},{9,8},{10,9},{11,10},{13,12},{... | collective-permute-start | bytes 6152 | tf_op jit(solution)/shard_map/ppermute | solution.py:16
  59.0 12.4 %collective-permute-start.8 = (f32[64,2,2,128]{3,0,2,1:T(8,128)S(1)}, f32[64,2,2,128]{3,0,2,1:T(8,128)S(1)}, u32[]{:S(2)}, u32[]{:S(2)}) collective-permute-start(f32[64,2,2,128]{3,0,2,1:T(8,128)S(1)} %bitcast_multiply_fusion.12), channel_id=1, source_target_pairs={{0,128},{1,129},{2,130},{3,131},{4,132},{5,133},{6,134},{7,135},{8... | collective-permute-start | bytes 393224 | tf_op jit(solution)/shard_map/ppermute | solution.py:24
  74.0 6.0 collective-permute-start.10
  80.2 9.0 %collective-permute-start.11 = (f32[64,2,4,1]{3,0,2,1:T(8,128)S(1)}, f32[64,2,4,1]{3,0,2,1:T(8,128)S(1)}, u32[]{:S(2)}, u32[]{:S(2)}) collective-permute-start(f32[64,2,4,1]{3,0,2,1:T(8,128)S(1)} %get-tuple-element.42), channel_id=1, source_target_pairs={{0,1},{1,2},{2,3},{4,5},{5,6},{6,7},{8,9},{9,10},{10,11},{12,13},{... | collective-permute-start | bytes 6152 | tf_op jit(solution)/shard_map/ppermute | solution.py:13
  82.2 9.0 %collective-permute-start.12 = (f32[64,2,4,1]{3,0,2,1:T(8,128)S(1)}, f32[64,2,4,1]{3,0,2,1:T(8,128)S(1)}, u32[]{:S(2)}, u32[]{:S(2)}) collective-permute-start(f32[64,2,4,1]{3,0,2,1:T(8,128)S(1)} %get-tuple-element.43), channel_id=1, source_target_pairs={{1,0},{2,1},{3,2},{5,4},{6,5},{7,6},{9,8},{10,9},{11,10},{13,12},{... | collective-permute-start | bytes 6152 | tf_op jit(solution)/shard_map/ppermute | solution.py:16
  96.2 5.1 collective-permute-start.13
  100.0 5.3 collective-permute-start.14
  105.5 9.0 %collective-permute-start.15 = (f32[64,2,4,1]{3,0,2,1:T(8,128)S(1)}, f32[64,2,4,1]{3,0,2,1:T(8,128)S(1)}, u32[]{:S(2)}, u32[]{:S(2)}) collective-permute-start(f32[64,2,4,1]{3,0,2,1:T(8,128)S(1)} %get-tuple-element.40), channel_id=1, source_target_pairs={{0,1},{1,2},{2,3},{4,5},{5,6},{6,7},{8,9},{9,10},{10,11},{12,13},{... | collective-permute-start | bytes 6152 | tf_op jit(solution)/shard_map/ppermute | solution.py:13
  107.7 9.3 %collective-permute-start.16 = (f32[64,2,4,1]{3,0,2,1:T(8,128)S(1)}, f32[64,2,4,1]{3,0,2,1:T(8,128)S(1)}, u32[]{:S(2)}, u32[]{:S(2)}) collective-permute-start(f32[64,2,4,1]{3,0,2,1:T(8,128)S(1)} %get-tuple-element.41), channel_id=1, source_target_pairs={{1,0},{2,1},{3,2},{5,4},{6,5},{7,6},{9,8},{10,9},{11,10},{13,12},{... | collective-permute-start | bytes 6152 | tf_op jit(solution)/shard_map/ppermute | solution.py:16
  122.2 11.4 %collective-permute-start.17 = (f32[64,2,2,128]{3,0,2,1:T(8,128)S(1)}, f32[64,2,2,128]{3,0,2,1:T(8,128)S(1)}, u32[]{:S(2)}, u32[]{:S(2)}) collective-permute-start(f32[64,2,2,128]{3,0,2,1:T(8,128)S(1)} %get-tuple-element.21), channel_id=1, source_target_pairs={{0,128},{1,129},{2,130},{3,131},{4,132},{5,133},{6,134},{7,135},{8... | collective-permute-start | bytes 393224 | tf_op jit(solution)/shard_map/ppermute | solution.py:24
  136.3 4.5 collective-permute-start.19
  141.0 9.0 %collective-permute-start.20 = (f32[64,2,4,1]{3,0,2,1:T(8,128)S(1)}, f32[64,2,4,1]{3,0,2,1:T(8,128)S(1)}, u32[]{:S(2)}, u32[]{:S(2)}) collective-permute-start(f32[64,2,4,1]{3,0,2,1:T(8,128)S(1)} %get-tuple-element.38), channel_id=1, source_target_pairs={{0,1},{1,2},{2,3},{4,5},{5,6},{6,7},{8,9},{9,10},{10,11},{12,13},{... | collective-permute-start | bytes 6152 | tf_op jit(solution)/shard_map/ppermute | solution.py:13
  143.2 9.3 %collective-permute-start.21 = (f32[64,2,4,1]{3,0,2,1:T(8,128)S(1)}, f32[64,2,4,1]{3,0,2,1:T(8,128)S(1)}, u32[]{:S(2)}, u32[]{:S(2)}) collective-permute-start(f32[64,2,4,1]{3,0,2,1:T(8,128)S(1)} %get-tuple-element.39), channel_id=1, source_target_pairs={{1,0},{2,1},{3,2},{5,4},{6,5},{7,6},{9,8},{10,9},{11,10},{13,12},{... | collective-permute-start | bytes 6152 | tf_op jit(solution)/shard_map/ppermute | solution.py:16
  157.6 4.8 collective-permute-start.22
  161.0 5.4 collective-permute-start.23
  166.6 9.0 %collective-permute-start.24 = (f32[64,2,4,1]{3,0,2,1:T(8,128)S(1)}, f32[64,2,4,1]{3,0,2,1:T(8,128)S(1)}, u32[]{:S(2)}, u32[]{:S(2)}) collective-permute-start(f32[64,2,4,1]{3,0,2,1:T(8,128)S(1)} %get-tuple-element.36), channel_id=1, source_target_pairs={{0,1},{1,2},{2,3},{4,5},{5,6},{6,7},{8,9},{9,10},{10,11},{12,13},{... | collective-permute-start | bytes 6152 | tf_op jit(solution)/shard_map/ppermute | solution.py:13
  168.5 9.0 %collective-permute-start.25 = (f32[64,2,4,1]{3,0,2,1:T(8,128)S(1)}, f32[64,2,4,1]{3,0,2,1:T(8,128)S(1)}, u32[]{:S(2)}, u32[]{:S(2)}) collective-permute-start(f32[64,2,4,1]{3,0,2,1:T(8,128)S(1)} %get-tuple-element.37), channel_id=1, source_target_pairs={{1,0},{2,1},{3,2},{5,4},{6,5},{7,6},{9,8},{10,9},{11,10},{13,12},{... | collective-permute-start | bytes 6152 | tf_op jit(solution)/shard_map/ppermute | solution.py:16
  182.8 5.1 collective-permute-start.26
  186.6 4.6 collective-permute-start.27
  191.3 9.0 %collective-permute-start.28 = (f32[64,2,4,1]{3,0,2,1:T(8,128)S(1)}, f32[64,2,4,1]{3,0,2,1:T(8,128)S(1)}, u32[]{:S(2)}, u32[]{:S(2)}) collective-permute-start(f32[64,2,4,1]{3,0,2,1:T(8,128)S(1)} %get-tuple-element.34), channel_id=1, source_target_pairs={{0,1},{1,2},{2,3},{4,5},{5,6},{6,7},{8,9},{9,10},{10,11},{12,13},{... | collective-permute-start | bytes 6152 | tf_op jit(solution)/shard_map/ppermute | solution.py:13
  193.3 9.0 %collective-permute-start.29 = (f32[64,2,4,1]{3,0,2,1:T(8,128)S(1)}, f32[64,2,4,1]{3,0,2,1:T(8,128)S(1)}, u32[]{:S(2)}, u32[]{:S(2)}) collective-permute-start(f32[64,2,4,1]{3,0,2,1:T(8,128)S(1)} %get-tuple-element.35), channel_id=1, source_target_pairs={{1,0},{2,1},{3,2},{5,4},{6,5},{7,6},{9,8},{10,9},{11,10},{13,12},{... | collective-permute-start | bytes 6152 | tf_op jit(solution)/shard_map/ppermute | solution.py:16
  207.2 5.1 collective-permute-start.30
  210.9 5.1 collective-permute-start.31
  216.2 9.0 %collective-permute-start.32 = (f32[64,2,4,1]{3,0,2,1:T(8,128)S(1)}, f32[64,2,4,1]{3,0,2,1:T(8,128)S(1)}, u32[]{:S(2)}, u32[]{:S(2)}) collective-permute-start(f32[64,2,4,1]{3,0,2,1:T(8,128)S(1)} %get-tuple-element.32), channel_id=1, source_target_pairs={{0,1},{1,2},{2,3},{4,5},{5,6},{6,7},{8,9},{9,10},{10,11},{12,13},{... | collective-permute-start | bytes 6152 | tf_op jit(solution)/shard_map/ppermute | solution.py:13
  218.2 9.1 %collective-permute-start.33 = (f32[64,2,4,1]{3,0,2,1:T(8,128)S(1)}, f32[64,2,4,1]{3,0,2,1:T(8,128)S(1)}, u32[]{:S(2)}, u32[]{:S(2)}) collective-permute-start(f32[64,2,4,1]{3,0,2,1:T(8,128)S(1)} %get-tuple-element.33), channel_id=1, source_target_pairs={{1,0},{2,1},{3,2},{5,4},{6,5},{7,6},{9,8},{10,9},{11,10},{13,12},{... | collective-permute-start | bytes 6152 | tf_op jit(solution)/shard_map/ppermute | solution.py:16
  231.9 11.5 %collective-permute-start.34 = (f32[64,2,2,128]{3,0,2,1:T(8,128)S(1)}, f32[64,2,2,128]{3,0,2,1:T(8,128)S(1)}, u32[]{:S(2)}, u32[]{:S(2)}) collective-permute-start(f32[64,2,2,128]{3,0,2,1:T(8,128)S(1)} %bitcast.1716), channel_id=1, source_target_pairs={{128,0},{129,1},{130,2},{131,3},{132,4},{133,5},{134,6},{135,7},{1... | collective-permute-start | bytes 393224 | tf_op jit(solution)/shard_map/ppermute | solution.py:24
  246.3 5.9 collective-permute-start.36
  252.4 9.0 %collective-permute-start.37 = (f32[64,2,4,1]{3,0,2,1:T(8,128)S(1)}, f32[64,2,4,1]{3,0,2,1:T(8,128)S(1)}, u32[]{:S(2)}, u32[]{:S(2)}) collective-permute-start(f32[64,2,4,1]{3,0,2,1:T(8,128)S(1)} %get-tuple-element.28), channel_id=1, source_target_pairs={{0,1},{1,2},{2,3},{4,5},{5,6},{6,7},{8,9},{9,10},{10,11},{12,13},{... | collective-permute-start | bytes 6152 | tf_op jit(solution)/shard_map/ppermute | solution.py:13
  254.8 9.3 %collective-permute-start.38 = (f32[64,2,4,1]{3,0,2,1:T(8,128)S(1)}, f32[64,2,4,1]{3,0,2,1:T(8,128)S(1)}, u32[]{:S(2)}, u32[]{:S(2)}) collective-permute-start(f32[64,2,4,1]{3,0,2,1:T(8,128)S(1)} %get-tuple-element.29), channel_id=1, source_target_pairs={{1,0},{2,1},{3,2},{5,4},{6,5},{7,6},{9,8},{10,9},{11,10},{13,12},{... | collective-permute-start | bytes 6152 | tf_op jit(solution)/shard_map/ppermute | solution.py:16
  269.0 5.7 collective-permute-start.39
  276.3 9.0 %collective-permute-start.41 = (f32[64,2,4,1]{3,0,2,1:T(8,128)S(1)}, f32[64,2,4,1]{3,0,2,1:T(8,128)S(1)}, u32[]{:S(2)}, u32[]{:S(2)}) collective-permute-start(f32[64,2,4,1]{3,0,2,1:T(8,128)S(1)} %get-tuple-element.26), channel_id=1, source_target_pairs={{0,1},{1,2},{2,3},{4,5},{5,6},{6,7},{8,9},{9,10},{10,11},{12,13},{... | collective-permute-start | bytes 6152 | tf_op jit(solution)/shard_map/ppermute | solution.py:13
  278.4 9.3 %collective-permute-start.42 = (f32[64,2,4,1]{3,0,2,1:T(8,128)S(1)}, f32[64,2,4,1]{3,0,2,1:T(8,128)S(1)}, u32[]{:S(2)}, u32[]{:S(2)}) collective-permute-start(f32[64,2,4,1]{3,0,2,1:T(8,128)S(1)} %get-tuple-element.27), channel_id=1, source_target_pairs={{1,0},{2,1},{3,2},{5,4},{6,5},{7,6},{9,8},{10,9},{11,10},{13,12},{... | collective-permute-start | bytes 6152 | tf_op jit(solution)/shard_map/ppermute | solution.py:16
  292.3 11.6 %collective-permute-start.43 = (f32[64,2,2,128]{3,0,2,1:T(8,128)S(1)}, f32[64,2,2,128]{3,0,2,1:T(8,128)S(1)}, u32[]{:S(2)}, u32[]{:S(2)}) collective-permute-start(f32[64,2,2,128]{3,0,2,1:T(8,128)S(1)} %bitcast.1715), channel_id=1, source_target_pairs={{128,0},{129,1},{130,2},{131,3},{132,4},{133,5},{134,6},{135,7},{1... | collective-permute-start | bytes 393224 | tf_op jit(solution)/shard_map/ppermute | solution.py:24
  307.1 6.7 collective-permute-start.44
  309.5 5.2 collective-permute-start.45
  314.8 9.0 %collective-permute-start.46 = (f32[64,2,4,1]{3,0,2,1:T(8,128)S(1)}, f32[64,2,4,1]{3,0,2,1:T(8,128)S(1)}, u32[]{:S(2)}, u32[]{:S(2)}) collective-permute-start(f32[64,2,4,1]{3,0,2,1:T(8,128)S(1)} %get-tuple-element.24), channel_id=1, source_target_pairs={{0,1},{1,2},{2,3},{4,5},{5,6},{6,7},{8,9},{9,10},{10,11},{12,13},{... | collective-permute-start | bytes 6152 | tf_op jit(solution)/shard_map/ppermute | solution.py:13
  316.8 9.0 %collective-permute-start.47 = (f32[64,2,4,1]{3,0,2,1:T(8,128)S(1)}, f32[64,2,4,1]{3,0,2,1:T(8,128)S(1)}, u32[]{:S(2)}, u32[]{:S(2)}) collective-permute-start(f32[64,2,4,1]{3,0,2,1:T(8,128)S(1)} %get-tuple-element.25), channel_id=1, source_target_pairs={{1,0},{2,1},{3,2},{5,4},{6,5},{7,6},{9,8},{10,9},{11,10},{13,12},{... | collective-permute-start | bytes 6152 | tf_op jit(solution)/shard_map/ppermute | solution.py:16
  335.1 342.8 %all-reduce.17.cloned.1.call-start = ((), (), s32[]{:S(2)}) async-start(), calls=%async_computation.1 | async-start | bytes 3538944 | tf_op jit(solution)/shard_map/psum | solution.py:147
  335.2 5.1 collective-permute-start.48
  339.0 4.9 collective-permute-start.49
  344.0 83.6 %collective-permute-start.50 = (f32[64,2,4,1]{3,0,2,1:T(8,128)S(1)}, f32[64,2,4,1]{3,0,2,1:T(8,128)S(1)}, u32[]{:S(2)}, u32[]{:S(2)}) collective-permute-start(f32[64,2,4,1]{3,0,2,1:T(8,128)S(1)} %get-tuple-element.22), channel_id=1, source_target_pairs={{0,1},{1,2},{2,3},{4,5},{5,6},{6,7},{8,9},{9,10},{10,11},{12,13},{... | collective-permute-start | bytes 6152 | tf_op jit(solution)/shard_map/ppermute | solution.py:13
  345.9 81.6 %collective-permute-start.51 = (f32[64,2,4,1]{3,0,2,1:T(8,128)S(1)}, f32[64,2,4,1]{3,0,2,1:T(8,128)}, u32[]{:S(2)}, u32[]{:S(2)}) collective-permute-start(f32[64,2,4,1]{3,0,2,1:T(8,128)S(1)} %get-tuple-element.23), channel_id=1, source_target_pairs={{1,0},{2,1},{3,2},{5,4},{6,5},{7,6},{9,8},{10,9},{11,10},{13,12},{... | collective-permute-start | bytes 6152 | tf_op jit(solution)/shard_map/ppermute | solution.py:16
  (10 other events, 222.6 us)
Sparse Core Ops, SparseCore 0:
  335.3 284.1 all-reduce.14
  622.0 55.9 all-reduce.16
